TPU v7x, 512 devices: a whole 4x4x16 slice. The times are simulated.
512 devices in a mesh: sa: 16 (over z_lo, core), sb: 16 (over y, x), noise: 2 (over z_hi).
Axes of the slice: x: 4, y: 4, z: 16 (z_hi: 2, z_lo: 8; z = z_hi * 8 + z_lo), core: 2. Of those that a mesh axis runs over, the one named last changes fastest.
Arguments:
- base: bfloat16 [8192, 1536], P(('sa', 'sb')), may hold values from -6 to 6
- noise: bfloat16 [4, 8192, 1536], P('noise', ('sa', 'sb')), may hold values from -3 to 3
- cot: bfloat16 [8192, 1536], P(('sa', 'sb')), may hold values from -6 to 6
- convolution_weight: bfloat16 [3, 1536, 384], P(None, 'sa'), may hold values from -0.15625 to 0.15625
- mix_w: bfloat16 [384, 1536], P('sa'), may hold values from -0.625 to 0.625
- norm_gain: float32 [1536], replicated, may hold values from 0.1 to 1.9
- qkv_w: bfloat16 [1536, 896], P('sa'), may hold values from -1 to 1
- out_w: bfloat16 [384, 1536], P('sa'), may hold values from -1.25 to 1.25
- band_width: int32 [4], replicated, may hold values from 1 to 32, as said below
- pairs: int32 [64, 2], replicated, may hold values from 0 to 63, as said below
Outputs:
- saliency: float32 [8192, 1536], P(('sa', 'sb'))
Inputs may be any that keep to these rules, and one draw needn't show every extreme that they name: `band_width`: one head has band half-width exactly 32. Tile t holds bins t * 128 to (t + 1) * 128 - 1; both tiles of a pair lie in the same stretch of 512 bins that starts at a multiple of 512; pairs may repeat.
All inputs are finite; a program needn't handle non-finite values.
Results may differ from a plain program's by a relative error of at most 0.018.
Values may be sent and summed in bfloat16 or wider, within the bound.
A program may use at most 64 MiB of HBM per device.

v0:
```python
import jax
import jax.numpy as jnp
from jax import lax
from jax.sharding import PartitionSpec as P

HID = 384
HEADS = 4
KEY = 64
VAL = 96
DILATION_BINS = 16
BAND = 32
TILE = 128
ROOT_TWO_PI = 0.7978845608
CUBIC = 0.044715


def extended(value, sides, width):
    for axis, dim in sides:
        peers, length = (lax.axis_size(axis), value.shape[dim])
        up = [(i, (i + 1) % peers) for i in range(peers - 1)]
        down = [(j, i) for i, j in up]
        last = lax.slice_in_dim(value, length - width, length, axis=dim)
        leading = lax.slice_in_dim(value, 0, width, axis=dim)
        before = lax.ppermute(last, axis, up)
        after = lax.ppermute(leading, axis, down)
        value = jnp.concatenate([before, value, after], axis=dim)
    return value


def from_behind(block, axis, distance):
    devices = range(lax.axis_size(axis))
    route = [(i - distance, i) for i in devices if i - distance in devices]
    return lax.ppermute(block, axis, route)


def gelu_tanh(values):
    inner = ROOT_TWO_PI * (values + CUBIC * values * values * values)
    return 0.5 * values * (1.0 + jnp.tanh(inner))


def gelu_slope(values):
    tangent = jnp.tanh(ROOT_TWO_PI * (values + CUBIC * values * values * values))
    return 0.5 * (1.0 + tangent) + 0.5 * values * (1.0 - tangent * tangent) * ROOT_TWO_PI * (
        1.0 + 3.0 * CUBIC * values * values
    )


def shards(base, noise, cot, convolution_weight, mix_w, norm_gain, qkv_w, out_w, band_width, pairs):
    conv_full, mix_full, qkv_full, out_full = (
        lax.all_gather(convolution_weight, "sa", axis=1, tiled=True),
        lax.all_gather(mix_w, "sa", axis=0, tiled=True),
        lax.all_gather(qkv_w, "sa", axis=0, tiled=True),
        lax.all_gather(out_w, "sa", axis=0, tiled=True),
    )
    sequence_bins = base.shape[0]
    samples_dev = noise.shape[0]
    stretch = sequence_bins * lax.axis_size("sb")
    sequence_length = stretch * lax.axis_size("sa")
    heads_key = HEADS * KEY
    heads_val = HEADS * VAL
    width = sequence_bins + 2 * BAND
    scale = KEY ** (-0.5)
    stretch_first = lax.axis_index("sa") * stretch
    first_row = stretch_first + lax.axis_index("sb") * sequence_bins
    row_pos = first_row + jnp.arange(sequence_bins, dtype=jnp.int32)
    ext_pos = first_row - BAND + jnp.arange(width, dtype=jnp.int32)
    stretch_pos = stretch_first + jnp.arange(stretch, dtype=jnp.int32)
    tiles = sequence_length // TILE
    tile_ids = jnp.arange(tiles, dtype=jnp.int32)
    pick_query = (pairs[:, 0][:, None] == tile_ids[None, :]).astype(jnp.float32)
    pick_key = (pairs[:, 1][:, None] == tile_ids[None, :]).astype(jnp.float32)
    table = jnp.dot(pick_query.T, pick_key)
    own_select = ((row_pos // TILE)[:, None] == tile_ids[None, :]).astype(jnp.float32)
    stretch_select = ((stretch_pos // TILE)[:, None] == tile_ids[None, :]).astype(jnp.float32)
    pair_own_rows = jnp.dot(jnp.dot(own_select, table), stretch_select.T) > 0.5
    pair_own_keys = jnp.dot(jnp.dot(stretch_select, table), own_select.T) > 0.5
    inside = (ext_pos >= 0) & (ext_pos < sequence_length)
    band_mask = inside[None, None, :] & (
        jnp.abs(row_pos[:, None] - ext_pos[None, :])[None] <= band_width[:, None, None]
    )
    far_rows = jnp.abs(row_pos[:, None] - stretch_pos[None, :])[None] > band_width[:, None, None]
    pair_mask = pair_own_rows[None] & far_rows
    key_mask = pair_own_keys[None] & jnp.transpose(far_rows, (0, 2, 1))
    noisy = base.astype(jnp.float32)[None] + noise.astype(jnp.float32)
    gelu_input = gelu_tanh(noisy).astype(jnp.bfloat16)
    gelu_extended = extended(gelu_input, ((("sa", "sb"), 1),), DILATION_BINS)
    hidden_state = jnp.zeros((samples_dev, sequence_bins, HID), jnp.float32)
    for tap_index in range(3):
        hidden_state = hidden_state + jnp.einsum(
            "nbd,dc->nbc",
            gelu_extended[:, tap_index * DILATION_BINS : tap_index * DILATION_BINS + sequence_bins],
            conv_full[tap_index],
            preferred_element_type=jnp.float32,
        )
    act = gelu_tanh(hidden_state).astype(jnp.bfloat16)
    resid = noisy + jnp.einsum("nbc,cd->nbd", act, mix_full, preferred_element_type=jnp.float32)
    inv_rms = lax.rsqrt(jnp.mean(resid * resid, axis=-1, keepdims=True) + 1e-06)
    normed = (resid * inv_rms * norm_gain).astype(jnp.bfloat16)
    proj = jnp.einsum("nbd,dc->nbc", normed, qkv_full, preferred_element_type=jnp.float32).astype(
        jnp.bfloat16
    )
    queries = proj[..., :heads_key].reshape(samples_dev, sequence_bins, HEADS, KEY)
    key_vals = proj[..., heads_key:]
    kv_ext = extended(key_vals, ((("sa", "sb"), 1),), BAND)
    kv_all = lax.all_gather(key_vals, "sb", axis=1, tiled=True)
    keys_ext = kv_ext[..., :heads_key].reshape(samples_dev, width, HEADS, KEY)
    vals_ext = kv_ext[..., heads_key:].reshape(samples_dev, width, HEADS, VAL)
    keys_all = kv_all[..., :heads_key].reshape(samples_dev, stretch, HEADS, KEY)
    vals_all = kv_all[..., heads_key:].reshape(samples_dev, stretch, HEADS, VAL)
    score_band = (
        jnp.einsum("nihd,njhd->nhij", queries, keys_ext, preferred_element_type=jnp.float32) * scale
    )
    score_band = jnp.where(band_mask[None], score_band, -1e30)
    raw_pair = jnp.einsum("nihd,njhd->nhij", queries, keys_all, preferred_element_type=jnp.float32)
    score_pair = jnp.where(pair_mask[None], raw_pair * scale, -1e30)
    top = jnp.maximum(jnp.max(score_band, axis=-1), jnp.max(score_pair, axis=-1))
    total = jnp.sum(jnp.where(band_mask[None], jnp.exp(score_band - top[..., None]), 0.0), axis=-1)
    total = total + jnp.sum(
        jnp.where(pair_mask[None], jnp.exp(score_pair - top[..., None]), 0.0), axis=-1
    )
    lse = top + jnp.log(total)
    prob_band = jnp.where(band_mask[None], jnp.exp(score_band - lse[..., None]), 0.0)
    prob_pair = jnp.where(pair_mask[None], jnp.exp(score_pair - lse[..., None]), 0.0)
    band_b = prob_band.astype(jnp.bfloat16)
    pair_b = prob_pair.astype(jnp.bfloat16)
    attn = jnp.einsum("nhij,njhe->nihe", band_b, vals_ext, preferred_element_type=jnp.float32)
    attn = attn + jnp.einsum(
        "nhij,njhe->nihe", pair_b, vals_all, preferred_element_type=jnp.float32
    )
    d_att = jnp.dot(cot, out_full.T, preferred_element_type=jnp.float32).astype(jnp.bfloat16)
    d_att_heads = d_att.reshape(sequence_bins, HEADS, VAL)
    delta = jnp.transpose(jnp.sum(d_att_heads.astype(jnp.float32)[None] * attn, axis=-1), (0, 2, 1))
    d_prob_band = jnp.einsum(
        "ihe,njhe->nhij", d_att_heads, vals_ext, preferred_element_type=jnp.float32
    )
    d_prob_pair = jnp.einsum(
        "ihe,njhe->nhij", d_att_heads, vals_all, preferred_element_type=jnp.float32
    )
    d_score_band = (prob_band * (d_prob_band - delta[..., None]) * scale).astype(jnp.bfloat16)
    d_score_pair = (prob_pair * (d_prob_pair - delta[..., None]) * scale).astype(jnp.bfloat16)
    d_query = jnp.einsum(
        "nhij,njhd->nihd", d_score_band, keys_ext, preferred_element_type=jnp.float32
    )
    d_query = d_query + jnp.einsum(
        "nhij,njhd->nihd", d_score_pair, keys_all, preferred_element_type=jnp.float32
    )
    d_key_ext = jnp.einsum(
        "nhij,nihd->njhd", d_score_band, queries, preferred_element_type=jnp.float32
    )
    d_val_ext = jnp.einsum(
        "nhij,ihe->njhe", band_b, d_att_heads, preferred_element_type=jnp.float32
    )
    d_kv_ext = jnp.concatenate(
        [
            d_key_ext.reshape(samples_dev, width, heads_key),
            d_val_ext.reshape(samples_dev, width, heads_val),
        ],
        axis=2,
    )
    from_right = from_behind(d_kv_ext[:, :BAND].astype(jnp.bfloat16), ("sa", "sb"), -1).astype(
        jnp.float32
    )
    from_left = from_behind(
        d_kv_ext[:, BAND + sequence_bins :].astype(jnp.bfloat16), ("sa", "sb"), 1
    ).astype(jnp.float32)
    d_key_vals = d_kv_ext[:, BAND : BAND + sequence_bins]
    d_key_vals = d_key_vals + from_left
    d_key_vals = d_key_vals + from_right
    statistics = jnp.stack([lse, delta], axis=1)
    query_rows = proj[..., :heads_key]
    queries_all, d_att_all = (
        lax.all_gather(query_rows, "sb", axis=1, tiled=True),
        lax.all_gather(d_att, "sb", axis=0, tiled=True),
    )
    stats_all = lax.all_gather(statistics, "sb", axis=3, tiled=True)
    queries_all = queries_all.reshape(samples_dev, stretch, HEADS, KEY)
    d_att_all = d_att_all.reshape(stretch, HEADS, VAL)
    keys_own = key_vals[..., :heads_key].reshape(samples_dev, sequence_bins, HEADS, KEY)
    vals_own = key_vals[..., heads_key:].reshape(samples_dev, sequence_bins, HEADS, VAL)
    score_key = (
        jnp.einsum("nihd,njhd->nhij", queries_all, keys_own, preferred_element_type=jnp.float32)
        * scale
    )
    prob_key = jnp.where(key_mask[None], jnp.exp(score_key - stats_all[:, 0][..., None]), 0.0)
    d_val_pair = jnp.einsum(
        "nhij,ihe->njhe",
        prob_key.astype(jnp.bfloat16),
        d_att_all,
        preferred_element_type=jnp.float32,
    )
    d_prob_key = jnp.einsum(
        "ihe,njhe->nhij", d_att_all, vals_own, preferred_element_type=jnp.float32
    )
    d_score_key = (prob_key * (d_prob_key - stats_all[:, 1][..., None]) * scale).astype(
        jnp.bfloat16
    )
    d_key_pair = jnp.einsum(
        "nhij,nihd->njhd", d_score_key, queries_all, preferred_element_type=jnp.float32
    )
    d_key_vals = d_key_vals + jnp.concatenate(
        [
            d_key_pair.reshape(samples_dev, sequence_bins, heads_key),
            d_val_pair.reshape(samples_dev, sequence_bins, heads_val),
        ],
        axis=2,
    )
    d_proj = jnp.concatenate(
        [d_query.reshape(samples_dev, sequence_bins, heads_key), d_key_vals], axis=2
    ).astype(jnp.bfloat16)
    d_normed = jnp.einsum("nbc,dc->nbd", d_proj, qkv_full, preferred_element_type=jnp.float32)
    gained = norm_gain * d_normed
    d_resid = (
        cot.astype(jnp.float32)[None]
        + inv_rms * gained
        - resid * inv_rms * inv_rms * inv_rms * jnp.mean(resid * gained, axis=-1, keepdims=True)
    )
    d_act = jnp.einsum(
        "nbd,cd->nbc", d_resid.astype(jnp.bfloat16), mix_full, preferred_element_type=jnp.float32
    )
    hidden_gradient = (d_act * gelu_slope(hidden_state)).astype(jnp.bfloat16)
    gradient_extended = extended(hidden_gradient, ((("sa", "sb"), 1),), DILATION_BINS)
    d_gelu_in = jnp.zeros((samples_dev, sequence_bins, base.shape[1]), jnp.float32)
    for tap_index in range(3):
        start_offset = (2 - tap_index) * DILATION_BINS
        d_gelu_in = d_gelu_in + jnp.einsum(
            "nbc,dc->nbd",
            gradient_extended[:, start_offset : start_offset + sequence_bins],
            conv_full[tap_index],
            preferred_element_type=jnp.float32,
        )
    grads = d_resid + d_gelu_in * gelu_slope(noisy)
    summed = lax.psum(jnp.sum(grads, axis=0).astype(jnp.bfloat16), "noise").astype(jnp.float32)
    return summed / (samples_dev * lax.axis_size("noise"))


def solution(mesh):
    return jax.shard_map(
        shards,
        mesh=mesh,
        in_specs=(
            P(("sa", "sb"), None),
            P("noise", ("sa", "sb"), None),
            P(("sa", "sb"), None),
            P(None, "sa", None),
            P("sa", None),
            P(),
            P("sa", None),
            P("sa", None),
            P(),
            P(),
        ),
        out_specs=P(("sa", "sb"), None),
        check_vma=False,
    )
```

profile of v0, /device:TPU:1, one launch (start us, length us, event | category | flops | bytes accessed | tf_op | source)
XLA Modules:
  0.0 632.5 jit_solution(18089078313766101049)
XLA Ops:
  10.9 8.2 %collective-permute-start.1 = (bf16[2,16,1536]{2,1,0:T(8,128)(2,1)S(1)}, bf16[2,16,1536]{2,1,0:T(8,128)(2,1)S(1)}, u32[]{:S(2)}, u32[]{:S(2)}) collective-permute-start(bf16[2,16,1536]{2,1,0:T(8,128)(2,1)S(1)} %get-tuple-element.10), channel_id=1, source_target_pairs={{2,0},{4,2},{6,4},{8,6},{10,8},{12,10},{14,12},{16,14},{18,16},{20... | collective-permute-start | bytes 294920 | tf_op jit(solution)/shard_map/ppermute | solution.py:25
  19.1 1.9 collective-permute-start
  22.6 95.0 %all-gather.6.cloned.1.call-done = bf16[3,1536,384]{2,1,0:T(8,128)(2,1)} async-done(((bf16[3,96,384]{2,1,0:T(8,128)(2,1)}), bf16[3,1536,384]{2,1,0:T(8,128)(2,1)}) %all-gather.6.cloned.1.call-update) | async-done | bytes 3538960 | tf_op jit(solution)/shard_map/all_gather | solution.py:50
  117.6 1.6 fusion.58
  119.2 1.6 fusion.60
  120.8 1.6 fusion.44
  122.4 97.1 %all-gather.8.cloned.1.call-done = bf16[384,1536]{1,0:T(8,128)(2,1)} async-done(((bf16[24,1536]{1,0:T(8,128)(2,1)}), bf16[384,1536]{1,0:T(8,128)(2,1)}) %all-gather.8.cloned.1.call-update) | async-done | bytes 1179664 | tf_op jit(solution)/shard_map/all_gather | solution.py:51
  219.5 1.7 multiply_reduce_fusion.1
  221.2 103.6 %all-gather.10.cloned.1.call-done = bf16[1536,896]{1,0:T(8,128)(2,1)} async-done(((bf16[96,896]{1,0:T(8,128)(2,1)}), bf16[1536,896]{1,0:T(8,128)(2,1)}) %all-gather.10.cloned.1.call-update) | async-done | bytes 2752528 | tf_op jit(solution)/shard_map/all_gather | solution.py:52
  324.9 2.4 fusion.28
  329.6 96.9 %all-gather.14.cloned.1.call-done = bf16[384,1536]{1,0:T(8,128)(2,1)} async-done(((bf16[24,1536]{1,0:T(8,128)(2,1)}), bf16[384,1536]{1,0:T(8,128)(2,1)}) %all-gather.14.cloned.1.call-update) | async-done | bytes 1179664 | tf_op jit(solution)/shard_map/all_gather | solution.py:53
  426.5 1.7 convolution_convert_fusion
  428.9 18.8 %all_gather.31 = bf16[512,384]{1,0:T(8,128)(2,1)S(1)} all-gather(bf16[32,384]{1,0:T(8,128)(2,1)S(1)} %convolution_convert_fusion), channel_id=1, replica_groups=mesh['sa'=16,'sb'=16,'noise'=2] {'sb'}, dimensions={0}, use_global_device_ids=true | all-gather | bytes 417792 | tf_op jit(solution)/shard_map/all_gather | solution.py:173
  447.9 2.7 collective-permute-start.2
  450.7 9.8 %collective-permute-start.3 = (bf16[2,32,640]{2,1,0:T(8,128)(2,1)S(1)}, bf16[2,32,640]{2,1,0:T(8,128)(2,1)S(1)}, u32[]{:S(2)}, u32[]{:S(2)}) collective-permute-start(bf16[2,32,640]{2,1,0:T(8,128)(2,1)S(1)} %copy-done.11), channel_id=1, source_target_pairs={{2,0},{4,2},{6,4},{8,6},{10,8},{12,10},{14,12},{16,14},{18,16},{20... | collective-permute-start | bytes 245768 | tf_op jit(solution)/shard_map/ppermute | solution.py:25
  460.6 16.1 %all_gather.29 = bf16[2,512,256]{2,1,0:T(8,128)(2,1)S(1)} all-gather(bf16[2,32,256]{2,1,0:T(8,128)(2,1)S(1)} %get-tuple-element.12), channel_id=1, replica_groups=mesh['sa'=16,'sb'=16,'noise'=2] {'sb'}, dimensions={1}, use_global_device_ids=true | all-gather | bytes 557056 | tf_op jit(solution)/shard_map/all_gather | solution.py:172
  479.7 9.0 %all-gather.12.cloned.1.call-done = bf16[2,512,640]{2,1,0:T(8,128)(2,1)} async-done(((bf16[2,32,640]{2,1,0:T(8,128)(2,1)}), bf16[2,512,640]{2,1,0:T(8,128)(2,1)}) %all-gather.12.cloned.1.call-update) | async-done | bytes 1310736 | tf_op jit(solution)/shard_map/all_gather | solution.py:105
  493.0 1.3 fusion.70
  495.3 1.9 fusion.26
  499.1 19.1 %all_gather.30 = f32[2,2,4,512]{2,1,0,3:T(2,128)S(1)} all-gather(f32[2,2,4,32]{2,1,0,3:T(2,128)S(1)} %copy.131), channel_id=1, replica_groups=mesh['sa'=16,'sb'=16,'noise'=2] {'sb'}, dimensions={3}, use_global_device_ids=true | all-gather | bytes 34816 | tf_op jit(solution)/shard_map/all_gather | solution.py:175
  521.9 2.0 collective-permute-start.4
  523.9 10.6 %collective-permute-start.5 = (bf16[2,32,640]{2,1,0:T(8,128)(2,1)}, bf16[2,32,640]{2,1,0:T(8,128)(2,1)}, u32[]{:S(2)}, u32[]{:S(2)}) collective-permute-start(bf16[2,32,640]{2,1,0:T(8,128)(2,1)} %get-tuple-element.8), channel_id=1, source_target_pairs={{2,0},{4,2},{6,4},{8,6},{10,8},{12,10},{14,12},{16,14},{18,16},{20... | collective-permute-start | bytes 245768 | tf_op jit(solution)/shard_map/ppermute | solution.py:33
  536.5 2.5 fusion.31
  541.0 1.6 copy.136
  542.6 1.7 reshape.252
  544.3 1.6 copy.138
  548.2 2.0 multiply_reduce_fusion
  550.7 1.9 collective-permute-start.7
  552.6 7.0 %collective-permute-start.6 = (bf16[2,16,384]{2,1,0:T(8,128)(2,1)S(1)}, bf16[2,16,384]{2,1,0:T(8,128)(2,1)S(1)}, u32[]{:S(2)}, u32[]{:S(2)}) collective-permute-start(bf16[2,16,384]{2,1,0:T(8,128)(2,1)S(1)} %get-tuple-element.13), channel_id=1, source_target_pairs={{2,0},{4,2},{6,4},{8,6},{10,8},{12,10},{14,12},{16,14},{18,16},{20... | collective-permute-start | bytes 73736 | tf_op jit(solution)/shard_map/ppermute | solution.py:25
  561.1 1.3 fusion.25
  562.4 61.6 %all-reduce.2.cloned.1.call-done = bf16[32,1536]{1,0:T(8,128)(2,1)} async-done(((bf16[32,1536]{1,0:T(8,128)(2,1)}), bf16[32,1536]{1,0:T(8,128)(2,1)}) %all-reduce.2.cloned.1.call-update) | async-done | bytes 98320 | tf_op jit(solution)/shard_map/psum | solution.py:232
  624.0 1.6 convert_multiply_fusion
  (174 shorter events, 30.9 us)
Async XLA Ops:
  6.5 14.7 %copy-start.40 = (s32[64,2]{0,1:T(2,128)S(1)}, s32[64,2]{0,1:T(2,128)}, u32[]{:S(2)}) copy-start(s32[64,2]{0,1:T(2,128)} %param.19) | copy-start | bytes 1540
  6.5 14.7 %copy-start.24 = (bf16[32,1536]{1,0:T(8,128)(2,1)S(1)}, bf16[32,1536]{1,0:T(8,128)(2,1)}, u32[]{:S(2)}) copy-start(bf16[32,1536]{1,0:T(8,128)(2,1)} %param.12) | copy-start | bytes 294916
  6.5 111.0 %all-gather.6.cloned.1.call-start = ((), (), s32[]{:S(2)}) async-start(), calls=%async_computation | async-start | bytes 3760128 | tf_op jit(solution)/shard_map/all_gather | solution.py:50
  7.3 212.3 %all-gather.8.cloned.1.call-start = ((), (), s32[]{:S(2)}) async-start(), calls=%async_computation.1 | async-start | bytes 1253376 | tf_op jit(solution)/shard_map/all_gather | solution.py:51
  8.0 316.8 %all-gather.10.cloned.1.call-start = ((), (), s32[]{:S(2)}) async-start(), calls=%async_computation.2 | async-start | bytes 2924544 | tf_op jit(solution)/shard_map/all_gather | solution.py:52
  8.7 417.7 %all-gather.14.cloned.1.call-start = ((), (), s32[]{:S(2)}) async-start(), calls=%async_computation.4 | async-start | bytes 1253376 | tf_op jit(solution)/shard_map/all_gather | solution.py:53
  9.7 209.8 %copy-start.8 = (f32[32,1536]{1,0:T(8,128)}, f32[32,1536]{1,0:T(8,128)S(1)}, u32[]{:S(2)}) copy-start(f32[32,1536]{1,0:T(8,128)S(1)} %convert_element_type.75) | copy-start | bytes 589828
  10.9 108.3 %collective-permute-start.1 = (bf16[2,16,1536]{2,1,0:T(8,128)(2,1)S(1)}, bf16[2,16,1536]{2,1,0:T(8,128)(2,1)S(1)}, u32[]{:S(2)}, u32[]{:S(2)}) collective-permute-start(bf16[2,16,1536]{2,1,0:T(8,128)(2,1)S(1)} %get-tuple-element.10), channel_id=1, source_target_pairs={{2,0},{4,2},{6,4},{8,6},{10,8},{12,10},{14,12},{16,14},{18,16},{20... | collective-permute-start | bytes 294920 | tf_op jit(solution)/shard_map/ppermute | solution.py:25
  19.1 101.7 %collective-permute-start = (bf16[2,16,1536]{2,1,0:T(8,128)(2,1)S(1)}, bf16[2,16,1536]{2,1,0:T(8,128)(2,1)S(1)}, u32[]{:S(2)}, u32[]{:S(2)}) collective-permute-start(bf16[2,16,1536]{2,1,0:T(8,128)(2,1)S(1)} %get-tuple-element.9), channel_id=1, source_target_pairs={{0,2},{2,4},{4,6},{6,8},{8,10},{10,12},{12,14},{14,16},{16,18},{18... | collective-permute-start | bytes 294920 | tf_op jit(solution)/shard_map/ppermute | solution.py:24
  21.1 467.6 %all-gather.12.cloned.1.call-start = ((), (), s32[]{:S(2)}) async-start(), calls=%async_computation.3 | async-start | bytes 1392640 | tf_op jit(solution)/shard_map/all_gather | solution.py:105
  120.8 98.8 %copy-start.20 = (bf16[2,32,1536]{2,1,0:T(8,128)(2,1)S(1)}, bf16[2,32,1536]{2,1,0:T(8,128)(2,1)}, u32[]{:S(2)}) copy-start(bf16[2,32,1536]{2,1,0:T(8,128)(2,1)} %param.11) | copy-start | bytes 589828
  122.4 204.9 %copy-start.17 = (f32[2,32,384]{2,1,0:T(8,128)}, f32[2,32,384]{2,1,0:T(8,128)S(1)}, u32[]{:S(2)}) copy-start(f32[2,32,384]{2,1,0:T(8,128)S(1)} %fusion.44) | copy-start | bytes 294916
  122.4 202.4 %copy-start.31 = (f32[1536]{0:T(1024)S(1)}, f32[1536]{0:T(1024)}, u32[]{:S(2)}) copy-start(f32[1536]{0:T(1024)} %param.15) | copy-start | bytes 18436
  221.2 106.1 %copy-start.37 = (f32[2,32]{1,0:T(2,128)}, f32[2,32]{1,0:T(2,128)S(1)}, u32[]{:S(2)}) copy-start(f32[2,32]{1,0:T(2,128)S(1)} %add_rsqrt_fusion) | copy-start | bytes 772
  327.3 133.1 %copy-start.19 = (bf16[2,32,896]{2,1,0:T(8,128)(2,1)}, bf16[2,32,896]{2,1,0:T(8,128)(2,1)S(1)}, u32[]{:S(2)}) copy-start(bf16[2,32,896]{2,1,0:T(8,128)(2,1)S(1)} %fusion.28) | copy-start | bytes 344068
  328.0 296.1 %all-reduce.2.cloned.1.call-start = ((), (), s32[]{:S(2)}) async-start(), calls=%async_computation.5 | async-start | bytes 196608 | tf_op jit(solution)/shard_map/psum | solution.py:232
  328.9 161.4 %copy-start.13 = (pred[4,32,512]{2,1,0:T(8,128)(4,1)}, pred[4,32,512]{2,1,0:T(8,128)(4,1)S(1)}, u32[]{:S(2)}) copy-start(pred[4,32,512]{2,1,0:T(8,128)(4,1)S(1)} %compare_and_fusion.1) | copy-start | bytes 196612
  329.6 118.3 %copy-start.11 = (bf16[2,32,640]{2,1,0:T(8,128)(2,1)S(1)}, bf16[2,32,640]{2,1,0:T(8,128)(2,1)}, u32[]{:S(2)}) copy-start(bf16[2,32,640]{2,1,0:T(8,128)(2,1)} %slice.121) | copy-start | bytes 245764
  428.3 19.4 %copy-start.25 = (bf16[32,4,96]{2,1,0:T(4,128)(2,1)}, bf16[32,4,96]{2,1,0:T(4,128)(2,1)S(1)}, u32[]{:S(2)}) copy-start(bf16[32,4,96]{2,1,0:T(4,128)(2,1)S(1)} %reshape.243) | copy-start | bytes 73732
  447.9 30.5 %collective-permute-start.2 = (bf16[2,32,640]{2,1,0:T(8,128)(2,1)S(1)}, bf16[2,32,640]{2,1,0:T(8,128)(2,1)S(1)}, u32[]{:S(2)}, u32[]{:S(2)}) collective-permute-start(bf16[2,32,640]{2,1,0:T(8,128)(2,1)S(1)} %copy-done.11), channel_id=1, source_target_pairs={{0,2},{2,4},{4,6},{6,8},{8,10},{10,12},{12,14},{14,16},{16,18},{18... | collective-permute-start | bytes 245768 | tf_op jit(solution)/shard_map/ppermute | solution.py:24
  450.7 27.8 %collective-permute-start.3 = (bf16[2,32,640]{2,1,0:T(8,128)(2,1)S(1)}, bf16[2,32,640]{2,1,0:T(8,128)(2,1)S(1)}, u32[]{:S(2)}, u32[]{:S(2)}) collective-permute-start(bf16[2,32,640]{2,1,0:T(8,128)(2,1)S(1)} %copy-done.11), channel_id=1, source_target_pairs={{2,0},{4,2},{6,4},{8,6},{10,8},{12,10},{14,12},{16,14},{18,16},{20... | collective-permute-start | bytes 245768 | tf_op jit(solution)/shard_map/ppermute | solution.py:25
  460.5 17.2 %slice-start.2 = ((bf16[2,32,896]{2,1,0:T(8,128)(2,1)}), bf16[2,32,384]{2,1,0:T(8,128)(2,1)S(1)}, s32[]{:S(2)}) async-start(bf16[2,32,896]{2,1,0:T(8,128)(2,1)} %copy-done.19), calls=%async_computation.8 | async-start | bytes 98304 | tf_op jit(solution)/shard_map/slice | solution.py:179
  460.6 29.4 %copy-start.15 = (bf16[2,32,4,64]{3,2,1,0:T(4,128)(2,1)}, bf16[2,32,4,64]{3,2,1,0:T(4,128)(2,1)S(1)}, u32[]{:S(2)}) copy-start(bf16[2,32,4,64]{3,2,1,0:T(4,128)(2,1)S(1)} %reshape.240) | copy-start | bytes 98308
  476.9 57.6 %copy-start.2 = (bf16[2,512,256]{1,2,0:T(8,128)(2,1)}, bf16[2,512,256]{1,2,0:T(8,128)(2,1)S(1)}, u32[]{:S(2)}) copy-start(bf16[2,512,256]{1,2,0:T(8,128)(2,1)S(1)} %copy.129) | copy-start | bytes 1572868
  498.2 21.8 %copy-start.30 = (bf16[2,4,32,96]{3,2,1,0:T(8,128)(2,1)}, bf16[2,4,32,96]{3,2,1,0:T(8,128)(2,1)S(1)}, u32[]{:S(2)}) copy-start(bf16[2,4,32,96]{3,2,1,0:T(8,128)(2,1)S(1)} %fusion.45) | copy-start | bytes 147460
  520.7 13.9 %copy-start.27 = (pred[4,512,32]{1,2,0:T(8,128)(4,1)S(1)}, pred[4,512,32]{1,2,0:T(8,128)(4,1)}, u32[]{:S(2)}) copy-start(pred[4,512,32]{1,2,0:T(8,128)(4,1)} %compare_and_fusion) | copy-start | bytes 196612
  521.1 14.5 %copy-start.4 = (f32[2,96,384]{2,1,0:T(8,128)}, f32[2,96,384]{2,1,0:T(8,128)S(1)}, u32[]{:S(2)}) copy-start(f32[2,96,384]{2,1,0:T(8,128)S(1)} %reshape.247) | copy-start | bytes 884740
  521.9 14.7 %copy-start.35 = (f32[2,4,512]{2,1,0:T(4,128)S(1)}, f32[2,4,512]{2,1,0:T(4,128)}, u32[]{:S(2)}) copy-start(f32[2,4,512]{2,1,0:T(4,128)} %copy.135) | copy-start | bytes 49156
  521.9 25.1 %collective-permute-start.4 = (bf16[2,32,640]{2,1,0:T(8,128)(2,1)}, bf16[2,32,640]{2,1,0:T(8,128)(2,1)}, u32[]{:S(2)}, u32[]{:S(2)}) collective-permute-start(bf16[2,32,640]{2,1,0:T(8,128)(2,1)} %get-tuple-element.7), channel_id=1, source_target_pairs={{0,2},{2,4},{4,6},{6,8},{8,10},{10,12},{12,14},{14,16},{16,18},{18... | collective-permute-start | bytes 245768 | tf_op jit(solution)/shard_map/ppermute | solution.py:33
  523.9 23.1 %collective-permute-start.5 = (bf16[2,32,640]{2,1,0:T(8,128)(2,1)}, bf16[2,32,640]{2,1,0:T(8,128)(2,1)}, u32[]{:S(2)}, u32[]{:S(2)}) collective-permute-start(bf16[2,32,640]{2,1,0:T(8,128)(2,1)} %get-tuple-element.8), channel_id=1, source_target_pairs={{2,0},{4,2},{6,4},{8,6},{10,8},{12,10},{14,12},{16,14},{18,16},{20... | collective-permute-start | bytes 245768 | tf_op jit(solution)/shard_map/ppermute | solution.py:33
  550.7 9.4 %collective-permute-start.7 = (bf16[2,16,384]{2,1,0:T(8,128)(2,1)S(1)}, bf16[2,16,384]{2,1,0:T(8,128)(2,1)S(1)}, u32[]{:S(2)}, u32[]{:S(2)}) collective-permute-start(bf16[2,16,384]{2,1,0:T(8,128)(2,1)S(1)} %get-tuple-element.14), channel_id=1, source_target_pairs={{0,2},{2,4},{4,6},{6,8},{8,10},{10,12},{12,14},{14,16},{16,18},{18... | collective-permute-start | bytes 73736 | tf_op jit(solution)/shard_map/ppermute | solution.py:24
  552.6 8.0 %collective-permute-start.6 = (bf16[2,16,384]{2,1,0:T(8,128)(2,1)S(1)}, bf16[2,16,384]{2,1,0:T(8,128)(2,1)S(1)}, u32[]{:S(2)}, u32[]{:S(2)}) collective-permute-start(bf16[2,16,384]{2,1,0:T(8,128)(2,1)S(1)} %get-tuple-element.13), channel_id=1, source_target_pairs={{2,0},{4,2},{6,4},{8,6},{10,8},{12,10},{14,12},{16,14},{18,16},{20... | collective-permute-start | bytes 73736 | tf_op jit(solution)/shard_map/ppermute | solution.py:25
  (26 other events, 106.2 us)
Sparse Core Ops, SparseCore 0:
  9.4 108.0 all-gather.5
  119.6 99.8 all-gather.7
  221.6 103.1 all-gather.9
  326.8 99.6 all-gather.13
  429.3 59.3 all-gather.11
  562.6 61.4 all-reduce.1
where the time goes:
time: 634 us; the launch traced here: 632 us
  waiting for transfers between devices  465 us (73%)
  blocking collectives  53.9 us (9%)
  starting transfers between devices  44.4 us (7%)
  matrix products  28.2 us (4%)
  local copies, waits for them, and re-layouts  16.6 us (3%)
  between operations  14.4 us (2%)
  other arithmetic  9.81 us (2%)
    all_gather x1, waiting for transfers between devices, shards(): lax.all_gather(qkv_w, 'sa', axis=0, tiled=True)  104 us
    all_gather x1, waiting for transfers between devices, shards(): lax.all_gather(mix_w, 'sa', axis=0, tiled=True)  97.1 us
    all_gather x1, waiting for transfers between devices, shards(): lax.all_gather(out_w, 'sa', axis=0, tiled=True)  96.9 us
    all_gather x1, waiting for transfers between devices, shards(): lax.all_gather(convolution_weight, 'sa', axis=1, tiled=True)  95 us
    psum x1, waiting for transfers between devices, shards(): lax.psum(jnp.sum(grads, axis=0).astype(jnp.bfloat16), 'noise')  61.6 us
    ppermute x3, starting transfers between devices, extended(): after = lax.ppermute(leading, axis, down)  25 us
    all_gather x1, blocking collectives, shards(): stats_all = lax.all_gather(statistics, 'sb', axis=3, tiled=True)  19.1 us
    all_gather x1, blocking collectives, shards(): lax.all_gather(d_att, 'sb', axis=0, tiled=True)  18.8 us
  transfers between devices with their start and end apart: 14, of which 6 were waited for; matrix products, arithmetic and copies ran while one was open for 5% of the time, Pallas kernels for 0%

commit v1 on v0

--- a/solution.py
+++ b/solution.py
@@ -48,7 +48,9 @@
 def shards(base, noise, cot, convolution_weight, mix_w, norm_gain, qkv_w, out_w, band_width, pairs):
     conv_full, mix_full, qkv_full, out_full = (
         lax.all_gather(convolution_weight, "sa", axis=1, tiled=True),
-        lax.all_gather(mix_w, "sa", axis=0, tiled=True),
+        jnp.concatenate(
+            lax.all_to_all(jnp.stack([mix_w] * lax.axis_size("sa")), "sa", 0, 0), axis=0
+        ),
         lax.all_gather(qkv_w, "sa", axis=0, tiled=True),
         lax.all_gather(out_w, "sa", axis=0, tiled=True),
     )

time: 634 us -> 541 us (0.85)
  waiting for transfers between devices: 465 us -> 364 us
  starting transfers between devices: 44.4 us -> 56.5 us
    all_gather x1 -> x0, waiting for transfers between devices: 97.1 us -> none  [shards(): lax.all_gather(mix_w, 'sa', axis=0, tiled=True)]
    all_to_all x0 -> x1, starting transfers between devices: none -> 14.2 us  [shards(): lax.all_to_all(jnp.stack([mix_w] * lax.axis_size('sa')), 'sa', 0, 0)]
  transfers between devices with their start and end apart: 14 -> 14, of which waited for: 6 -> 5; matrix products, arithmetic and copies ran while one was open for 5% -> 6% of each run, Pallas kernels for 0% -> 0%
where the time goes in v1:
time: 541 us; the launch traced here: 540 us
  waiting for transfers between devices  364 us (67%)
  starting transfers between devices  56.5 us (10%)
  blocking collectives  53.5 us (10%)
  matrix products  27 us (5%)
  local copies, waits for them, and re-layouts  17.9 us (3%)
  between operations  14.1 us (3%)
  other arithmetic  7.19 us (1%)
    all_gather x1, waiting for transfers between devices, shards(): lax.all_gather(qkv_w, 'sa', axis=0, tiled=True)  103 us
    all_gather x1, waiting for transfers between devices, shards(): lax.all_gather(out_w, 'sa', axis=0, tiled=True)  97 us
    all_gather x1, waiting for transfers between devices, shards(): lax.all_gather(convolution_weight, 'sa', axis=1, tiled=True)  92.7 us
    psum x1, waiting for transfers between devices, shards(): lax.psum(jnp.sum(grads, axis=0).astype(jnp.bfloat16), 'noise')  61 us
    ppermute x3, starting transfers between devices, extended(): after = lax.ppermute(leading, axis, down)  26.3 us
    all_gather x1, blocking collectives, shards(): lax.all_gather(d_att, 'sb', axis=0, tiled=True)  18.8 us
    all_gather x1, blocking collectives, shards(): stats_all = lax.all_gather(statistics, 'sb', axis=3, tiled=True)  18.7 us
    all_gather x1, blocking collectives, shards(): lax.all_gather(query_rows, 'sb', axis=1, tiled=True)  16.1 us
  transfers between devices with their start and end apart: 14, of which 5 were waited for; matrix products, arithmetic and copies ran while one was open for 6% of the time, Pallas kernels for 0%

profile of v1, /device:TPU:1, one launch (start us, length us, event | category | flops | bytes accessed | tf_op | source)
XLA Modules:
  0.0 540.3 jit_solution(2844569509269740087)
XLA Ops:
  8.0 2.0 stack.6
  10.0 14.2 %all-to-all-start = ((bf16[16,24,1536]{2,1,0:T(8,128)(2,1)}), bf16[16,24,1536]{2,1,0:T(8,128)(2,1)S(1)}, u32[]{:S(2)}, u32[]{:S(2)}) async-start(bf16[16,24,1536]{2,1,0:T(8,128)(2,1)} %stack.6), calls=%async_computation | async-start | bytes 2359296 | tf_op jit(solution)/shard_map/all_to_all | solution.py:52
  24.5 6.8 %collective-permute-start.1 = (bf16[2,16,1536]{2,1,0:T(8,128)(2,1)S(1)}, bf16[2,16,1536]{2,1,0:T(8,128)(2,1)S(1)}, u32[]{:S(2)}, u32[]{:S(2)}) collective-permute-start(bf16[2,16,1536]{2,1,0:T(8,128)(2,1)S(1)} %get-tuple-element.10), channel_id=1, source_target_pairs={{2,0},{4,2},{6,4},{8,6},{10,8},{12,10},{14,12},{16,14},{18,16},{20... | collective-permute-start | bytes 294920 | tf_op jit(solution)/shard_map/ppermute | solution.py:25
  31.3 1.9 collective-permute-start
  34.8 92.7 %all-gather.5.cloned.1.call-done = bf16[3,1536,384]{2,1,0:T(8,128)(2,1)} async-done(((bf16[3,96,384]{2,1,0:T(8,128)(2,1)}), bf16[3,1536,384]{2,1,0:T(8,128)(2,1)}) %all-gather.5.cloned.1.call-update) | async-done | bytes 3538960 | tf_op jit(solution)/shard_map/all_gather | solution.py:50
  127.4 1.6 fusion.50
  129.0 1.6 fusion.52
  130.6 1.6 fusion.38
  132.7 102.9 %all-gather.7.cloned.1.call-done = bf16[1536,896]{1,0:T(8,128)(2,1)} async-done(((bf16[96,896]{1,0:T(8,128)(2,1)}), bf16[1536,896]{1,0:T(8,128)(2,1)}) %all-gather.7.cloned.1.call-update) | async-done | bytes 2752528 | tf_op jit(solution)/shard_map/all_gather | solution.py:54
  235.6 2.4 fusion.25
  240.3 97.0 %all-gather.11.cloned.1.call-done = bf16[384,1536]{1,0:T(8,128)(2,1)} async-done(((bf16[24,1536]{1,0:T(8,128)(2,1)}), bf16[384,1536]{1,0:T(8,128)(2,1)}) %all-gather.11.cloned.1.call-update) | async-done | bytes 1179664 | tf_op jit(solution)/shard_map/all_gather | solution.py:55
  337.3 1.7 convolution_convert_fusion
  339.8 18.8 %all_gather.27 = bf16[512,384]{1,0:T(8,128)(2,1)S(1)} all-gather(bf16[32,384]{1,0:T(8,128)(2,1)S(1)} %convolution_convert_fusion), channel_id=1, replica_groups=mesh['sa'=16,'sb'=16,'noise'=2] {'sb'}, dimensions={0}, use_global_device_ids=true | all-gather | bytes 417792 | tf_op jit(solution)/shard_map/all_gather | solution.py:175
  358.8 2.7 collective-permute-start.2
  361.5 9.8 %collective-permute-start.3 = (bf16[2,32,640]{2,1,0:T(8,128)(2,1)S(1)}, bf16[2,32,640]{2,1,0:T(8,128)(2,1)S(1)}, u32[]{:S(2)}, u32[]{:S(2)}) collective-permute-start(bf16[2,32,640]{2,1,0:T(8,128)(2,1)S(1)} %copy-done.12), channel_id=1, source_target_pairs={{2,0},{4,2},{6,4},{8,6},{10,8},{12,10},{14,12},{16,14},{18,16},{20... | collective-permute-start | bytes 245768 | tf_op jit(solution)/shard_map/ppermute | solution.py:25
  371.5 16.1 %all_gather.25 = bf16[2,512,256]{2,1,0:T(8,128)(2,1)S(1)} all-gather(bf16[2,32,256]{2,1,0:T(8,128)(2,1)S(1)} %get-tuple-element.12), channel_id=1, replica_groups=mesh['sa'=16,'sb'=16,'noise'=2] {'sb'}, dimensions={1}, use_global_device_ids=true | all-gather | bytes 557056 | tf_op jit(solution)/shard_map/all_gather | solution.py:174
  390.5 9.0 %all-gather.9.cloned.1.call-done = bf16[2,512,640]{2,1,0:T(8,128)(2,1)} async-done(((bf16[2,32,640]{2,1,0:T(8,128)(2,1)}), bf16[2,512,640]{2,1,0:T(8,128)(2,1)}) %all-gather.9.cloned.1.call-update) | async-done | bytes 1310736 | tf_op jit(solution)/shard_map/all_gather | solution.py:107
  403.9 1.3 fusion.62
  406.2 1.9 fusion.23
  411.2 2.6 collective-permute-start.4
  413.8 6.3 %collective-permute-start.5 = (bf16[2,32,640]{2,1,0:T(8,128)(2,1)}, bf16[2,32,640]{2,1,0:T(8,128)(2,1)}, u32[]{:S(2)}, u32[]{:S(2)}) collective-permute-start(bf16[2,32,640]{2,1,0:T(8,128)(2,1)} %get-tuple-element.8), channel_id=1, source_target_pairs={{2,0},{4,2},{6,4},{8,6},{10,8},{12,10},{14,12},{16,14},{18,16},{20... | collective-permute-start | bytes 245768 | tf_op jit(solution)/shard_map/ppermute | solution.py:33
  420.2 18.7 %all_gather.26 = f32[2,2,4,512]{2,1,0,3:T(2,128)S(1)} all-gather(f32[2,2,4,32]{2,1,0,3:T(2,128)S(1)} %copy.131), channel_id=1, replica_groups=mesh['sa'=16,'sb'=16,'noise'=2] {'sb'}, dimensions={3}, use_global_device_ids=true | all-gather | bytes 34816 | tf_op jit(solution)/shard_map/all_gather | solution.py:177
  442.1 2.5 fusion.28
  446.6 1.6 copy.136
  448.2 1.7 reshape.258
  449.9 1.6 copy.138
  453.7 2.0 multiply_reduce_fusion
  456.3 2.3 collective-permute-start.7
  458.6 9.7 %collective-permute-start.6 = (bf16[2,16,384]{2,1,0:T(8,128)(2,1)S(1)}, bf16[2,16,384]{2,1,0:T(8,128)(2,1)S(1)}, u32[]{:S(2)}, u32[]{:S(2)}) collective-permute-start(bf16[2,16,384]{2,1,0:T(8,128)(2,1)S(1)} %get-tuple-element.13), channel_id=1, source_target_pairs={{2,0},{4,2},{6,4},{8,6},{10,8},{12,10},{14,12},{16,14},{18,16},{20... | collective-permute-start | bytes 73736 | tf_op jit(solution)/shard_map/ppermute | solution.py:25
  469.8 1.3 fusion.22
  471.2 61.0 %all-reduce.2.cloned.1.call-done = bf16[32,1536]{1,0:T(8,128)(2,1)} async-done(((bf16[32,1536]{1,0:T(8,128)(2,1)}), bf16[32,1536]{1,0:T(8,128)(2,1)}) %all-reduce.2.cloned.1.call-update) | async-done | bytes 98320 | tf_op jit(solution)/shard_map/psum | solution.py:234
  532.2 1.6 convert_multiply_fusion
  (178 shorter events, 27.5 us)
Async XLA Ops:
  6.5 120.9 %all-gather.5.cloned.1.call-start = ((), (), s32[]{:S(2)}) async-start(), calls=%async_computation.1 | async-start | bytes 3760128 | tf_op jit(solution)/shard_map/all_gather | solution.py:50
  7.3 228.3 %all-gather.7.cloned.1.call-start = ((), (), s32[]{:S(2)}) async-start(), calls=%async_computation.2 | async-start | bytes 2924544 | tf_op jit(solution)/shard_map/all_gather | solution.py:54
  10.0 14.2 %copy-start.36 = (bf16[32,1536]{1,0:T(8,128)(2,1)S(1)}, bf16[32,1536]{1,0:T(8,128)(2,1)}, u32[]{:S(2)}) copy-start(bf16[32,1536]{1,0:T(8,128)(2,1)} %param.10) | copy-start | bytes 294916
  10.0 14.3 %copy-start.21 = (bf16[2,32,1536]{2,1,0:T(8,128)(2,1)S(1)}, bf16[2,32,1536]{2,1,0:T(8,128)(2,1)}, u32[]{:S(2)}) copy-start(bf16[2,32,1536]{2,1,0:T(8,128)(2,1)} %param.11) | copy-start | bytes 589828
  10.0 122.2 %all-to-all-start = ((bf16[16,24,1536]{2,1,0:T(8,128)(2,1)}), bf16[16,24,1536]{2,1,0:T(8,128)(2,1)S(1)}, u32[]{:S(2)}, u32[]{:S(2)}) async-start(bf16[16,24,1536]{2,1,0:T(8,128)(2,1)} %stack.6), calls=%async_computation | async-start | bytes 2359296 | tf_op jit(solution)/shard_map/all_to_all | solution.py:52
  24.2 313.1 %all-gather.11.cloned.1.call-start = ((), (), s32[]{:S(2)}) async-start(), calls=%async_computation.4 | async-start | bytes 1253376 | tf_op jit(solution)/shard_map/all_gather | solution.py:55
  24.3 108.0 %copy-start.9 = (f32[32,1536]{1,0:T(8,128)}, f32[32,1536]{1,0:T(8,128)S(1)}, u32[]{:S(2)}) copy-start(f32[32,1536]{1,0:T(8,128)S(1)} %convert_element_type.75) | copy-start | bytes 589828
  24.5 104.5 %collective-permute-start.1 = (bf16[2,16,1536]{2,1,0:T(8,128)(2,1)S(1)}, bf16[2,16,1536]{2,1,0:T(8,128)(2,1)S(1)}, u32[]{:S(2)}, u32[]{:S(2)}) collective-permute-start(bf16[2,16,1536]{2,1,0:T(8,128)(2,1)S(1)} %get-tuple-element.10), channel_id=1, source_target_pairs={{2,0},{4,2},{6,4},{8,6},{10,8},{12,10},{14,12},{16,14},{18,16},{20... | collective-permute-start | bytes 294920 | tf_op jit(solution)/shard_map/ppermute | solution.py:25
  31.3 99.3 %collective-permute-start = (bf16[2,16,1536]{2,1,0:T(8,128)(2,1)S(1)}, bf16[2,16,1536]{2,1,0:T(8,128)(2,1)S(1)}, u32[]{:S(2)}, u32[]{:S(2)}) collective-permute-start(bf16[2,16,1536]{2,1,0:T(8,128)(2,1)S(1)} %get-tuple-element.9), channel_id=1, source_target_pairs={{0,2},{2,4},{4,6},{6,8},{8,10},{10,12},{12,14},{14,16},{16,18},{18... | collective-permute-start | bytes 294920 | tf_op jit(solution)/shard_map/ppermute | solution.py:24
  33.3 366.3 %all-gather.9.cloned.1.call-start = ((), (), s32[]{:S(2)}) async-start(), calls=%async_computation.3 | async-start | bytes 1392640 | tf_op jit(solution)/shard_map/all_gather | solution.py:107
  132.2 105.8 %copy-start.18 = (f32[2,32,384]{2,1,0:T(8,128)}, f32[2,32,384]{2,1,0:T(8,128)S(1)}, u32[]{:S(2)}) copy-start(f32[2,32,384]{2,1,0:T(8,128)S(1)} %fusion.38) | copy-start | bytes 294916
  132.2 103.3 %copy-start.32 = (f32[1536]{0:T(1024)S(1)}, f32[1536]{0:T(1024)}, u32[]{:S(2)}) copy-start(f32[1536]{0:T(1024)} %param.15) | copy-start | bytes 18436
  132.3 105.8 %copy-start.1 = (bf16[16,24,1536]{2,1,0:T(8,128)(2,1)}, bf16[16,24,1536]{2,1,0:T(8,128)(2,1)S(1)}, u32[]{:S(2)}) copy-start(bf16[16,24,1536]{2,1,0:T(8,128)(2,1)S(1)} %all-to-all-done) | copy-start | bytes 3538948
  132.7 105.3 %copy-start.38 = (f32[2,32]{1,0:T(2,128)}, f32[2,32]{1,0:T(2,128)S(1)}, u32[]{:S(2)}) copy-start(f32[2,32]{1,0:T(2,128)S(1)} %add_rsqrt_fusion) | copy-start | bytes 772
  238.0 133.3 %copy-start.20 = (bf16[2,32,896]{2,1,0:T(8,128)(2,1)}, bf16[2,32,896]{2,1,0:T(8,128)(2,1)S(1)}, u32[]{:S(2)}) copy-start(bf16[2,32,896]{2,1,0:T(8,128)(2,1)S(1)} %fusion.25) | copy-start | bytes 344068
  238.7 293.5 %all-reduce.2.cloned.1.call-start = ((), (), s32[]{:S(2)}) async-start(), calls=%async_computation.5 | async-start | bytes 196608 | tf_op jit(solution)/shard_map/psum | solution.py:234
  239.6 161.6 %copy-start.14 = (pred[4,32,512]{2,1,0:T(8,128)(4,1)}, pred[4,32,512]{2,1,0:T(8,128)(4,1)S(1)}, u32[]{:S(2)}) copy-start(pred[4,32,512]{2,1,0:T(8,128)(4,1)S(1)} %compare_and_fusion.1) | copy-start | bytes 196612
  240.3 118.4 %copy-start.12 = (bf16[2,32,640]{2,1,0:T(8,128)(2,1)S(1)}, bf16[2,32,640]{2,1,0:T(8,128)(2,1)}, u32[]{:S(2)}) copy-start(bf16[2,32,640]{2,1,0:T(8,128)(2,1)} %slice.121) | copy-start | bytes 245764
  339.2 32.1 %copy-start.26 = (bf16[32,4,96]{2,1,0:T(4,128)(2,1)}, bf16[32,4,96]{2,1,0:T(4,128)(2,1)S(1)}, u32[]{:S(2)}) copy-start(bf16[32,4,96]{2,1,0:T(4,128)(2,1)S(1)} %reshape.249) | copy-start | bytes 73732
  358.8 30.5 %collective-permute-start.2 = (bf16[2,32,640]{2,1,0:T(8,128)(2,1)S(1)}, bf16[2,32,640]{2,1,0:T(8,128)(2,1)S(1)}, u32[]{:S(2)}, u32[]{:S(2)}) collective-permute-start(bf16[2,32,640]{2,1,0:T(8,128)(2,1)S(1)} %copy-done.12), channel_id=1, source_target_pairs={{0,2},{2,4},{4,6},{6,8},{8,10},{10,12},{12,14},{14,16},{16,18},{18... | collective-permute-start | bytes 245768 | tf_op jit(solution)/shard_map/ppermute | solution.py:24
  361.5 27.8 %collective-permute-start.3 = (bf16[2,32,640]{2,1,0:T(8,128)(2,1)S(1)}, bf16[2,32,640]{2,1,0:T(8,128)(2,1)S(1)}, u32[]{:S(2)}, u32[]{:S(2)}) collective-permute-start(bf16[2,32,640]{2,1,0:T(8,128)(2,1)S(1)} %copy-done.12), channel_id=1, source_target_pairs={{2,0},{4,2},{6,4},{8,6},{10,8},{12,10},{14,12},{16,14},{18,16},{20... | collective-permute-start | bytes 245768 | tf_op jit(solution)/shard_map/ppermute | solution.py:25
  371.4 17.2 %slice-start.2 = ((bf16[2,32,896]{2,1,0:T(8,128)(2,1)}), bf16[2,32,384]{2,1,0:T(8,128)(2,1)S(1)}, s32[]{:S(2)}) async-start(bf16[2,32,896]{2,1,0:T(8,128)(2,1)} %copy-done.20), calls=%async_computation.8 | async-start | bytes 98304 | tf_op jit(solution)/shard_map/slice | solution.py:181
  371.5 29.4 %copy-start.16 = (bf16[2,32,4,64]{3,2,1,0:T(4,128)(2,1)}, bf16[2,32,4,64]{3,2,1,0:T(4,128)(2,1)S(1)}, u32[]{:S(2)}) copy-start(bf16[2,32,4,64]{3,2,1,0:T(4,128)(2,1)S(1)} %reshape.246) | copy-start | bytes 98308
  387.8 52.4 %copy-start.3 = (bf16[2,512,256]{1,2,0:T(8,128)(2,1)}, bf16[2,512,256]{1,2,0:T(8,128)(2,1)S(1)}, u32[]{:S(2)}) copy-start(bf16[2,512,256]{1,2,0:T(8,128)(2,1)S(1)} %copy.129) | copy-start | bytes 1572868
  389.4 11.4 %copy-start.13 = (bf16[2,96,256]{1,2,0:T(8,128)(2,1)}, bf16[2,96,256]{1,2,0:T(8,128)(2,1)S(1)}, u32[]{:S(2)}) copy-start(bf16[2,96,256]{1,2,0:T(8,128)(2,1)S(1)} %copy.113) | copy-start | bytes 294916
  410.4 29.3 %copy-start.5 = (f32[2,96,384]{2,1,0:T(8,128)}, f32[2,96,384]{2,1,0:T(8,128)S(1)}, u32[]{:S(2)}) copy-start(f32[2,96,384]{2,1,0:T(8,128)S(1)} %reshape.253) | copy-start | bytes 884740
  411.2 41.4 %collective-permute-start.4 = (bf16[2,32,640]{2,1,0:T(8,128)(2,1)}, bf16[2,32,640]{2,1,0:T(8,128)(2,1)}, u32[]{:S(2)}, u32[]{:S(2)}) collective-permute-start(bf16[2,32,640]{2,1,0:T(8,128)(2,1)} %get-tuple-element.7), channel_id=1, source_target_pairs={{0,2},{2,4},{4,6},{6,8},{8,10},{10,12},{12,14},{14,16},{16,18},{18... | collective-permute-start | bytes 245768 | tf_op jit(solution)/shard_map/ppermute | solution.py:33
  413.8 38.8 %collective-permute-start.5 = (bf16[2,32,640]{2,1,0:T(8,128)(2,1)}, bf16[2,32,640]{2,1,0:T(8,128)(2,1)}, u32[]{:S(2)}, u32[]{:S(2)}) collective-permute-start(bf16[2,32,640]{2,1,0:T(8,128)(2,1)} %get-tuple-element.8), channel_id=1, source_target_pairs={{2,0},{4,2},{6,4},{8,6},{10,8},{12,10},{14,12},{16,14},{18,16},{20... | collective-permute-start | bytes 245768 | tf_op jit(solution)/shard_map/ppermute | solution.py:33
  442.1 11.6 %copy-start = (bf16[1536,896]{1,0:T(8,128)(2,1)S(1)}, bf16[1536,896]{1,0:T(8,128)(2,1)}, u32[]{:S(2)}) copy-start(bf16[1536,896]{1,0:T(8,128)(2,1)} %all-gather.7.cloned.1.call-done) | copy-start | bytes 8257540
  453.7 14.6 %copy-start.4 = (bf16[3,1536,384]{2,1,0:T(8,128)(2,1)S(1)}, bf16[3,1536,384]{2,1,0:T(8,128)(2,1)}, u32[]{:S(2)}) copy-start(bf16[3,1536,384]{2,1,0:T(8,128)(2,1)} %all-gather.5.cloned.1.call-done) | copy-start | bytes 10616836
  456.3 12.6 %collective-permute-start.7 = (bf16[2,16,384]{2,1,0:T(8,128)(2,1)S(1)}, bf16[2,16,384]{2,1,0:T(8,128)(2,1)S(1)}, u32[]{:S(2)}, u32[]{:S(2)}) collective-permute-start(bf16[2,16,384]{2,1,0:T(8,128)(2,1)S(1)} %get-tuple-element.14), channel_id=1, source_target_pairs={{0,2},{2,4},{4,6},{6,8},{8,10},{10,12},{12,14},{14,16},{16,18},{18... | collective-permute-start | bytes 73736 | tf_op jit(solution)/shard_map/ppermute | solution.py:24
  458.6 10.7 %collective-permute-start.6 = (bf16[2,16,384]{2,1,0:T(8,128)(2,1)S(1)}, bf16[2,16,384]{2,1,0:T(8,128)(2,1)S(1)}, u32[]{:S(2)}, u32[]{:S(2)}) collective-permute-start(bf16[2,16,384]{2,1,0:T(8,128)(2,1)S(1)} %get-tuple-element.13), channel_id=1, source_target_pairs={{2,0},{4,2},{6,4},{8,6},{10,8},{12,10},{14,12},{16,14},{18,16},{20... | collective-permute-start | bytes 73736 | tf_op jit(solution)/shard_map/ppermute | solution.py:25
  (28 other events, 84.7 us)
Sparse Core Ops, SparseCore 0:
  9.4 117.9 all-gather.4
  129.5 106.0 all-gather.6
  237.7 99.6 all-gather.10
  340.2 59.3 all-gather.8
  471.3 60.8 all-reduce.1
